TPU v7x, 256 devices: a whole 4x4x8 slice. The times are simulated.
256 devices in a mesh: ctx: 256 (over y, z, x, core).
Axes of the slice: x: 4, y: 4, z: 8, core: 2. Of those that a mesh axis runs over, the one named last changes fastest.
Arguments:
- queries: bfloat16 [65536, 768], P('ctx'), may hold values from -16 to 16
- keys: bfloat16 [65536, 768], P('ctx'), may hold values from -16 to 16
- values: bfloat16 [65536, 768], P('ctx'), may hold values from -6 to 6
- offsets: int32 [5, 12], replicated, may hold values from 0 to 255, as said below
Outputs:
- attended: bfloat16 [65536, 768], P('ctx')
Inputs may be any that keep to these rules, and one draw needn't show every extreme that they name: offsets[l, h] lies in 0 to min(4 ** l, 256) - 1.
All inputs are finite; a program needn't handle non-finite values.
Results may differ from a plain program's by a relative error of at most 0.0035.
Values may be sent and summed in bfloat16 or wider, within the bound.
No kernel may reach another device: no remote copies, remote signals or barrier semaphores. Data moves between devices by JAX's collectives and lax.ppermute only.
A program may use at most 64 MiB of HBM per device.

v0:
```python
import functools

import jax
import jax.numpy as jnp
from jax import lax
from jax.experimental import pallas as pl
from jax.experimental.pallas import tpu as pltpu
from jax.sharding import PartitionSpec as P

HEADS = 12
PAIRS = 6
LANES = 128
HALF = 64
TOK = 256
WIDTH = 768
NEG = -1e30
SCALE = 0.125
F32 = jnp.float32
BF16 = jnp.bfloat16
SEL = 96
STAT = 16
VMEM = pl.BlockSpec(memory_space=pltpu.VMEM)
SMEM = pl.BlockSpec(memory_space=pltpu.SMEM)


def iota(shape, dim):
    return lax.broadcasted_iota(jnp.int32, shape, dim)


def dot_nt(a, b):
    return lax.dot_general(a, b, (((1,), (1,)), ((), ())), preferred_element_type=F32)


def dot_nn(a, b):
    return jnp.dot(a, b, preferred_element_type=F32)


def lanes_of(pair):
    return slice(pair * LANES, (pair + 1) * LANES)


def split_heads(rows):
    low = iota(rows.shape, 1) < HALF
    zero = jnp.zeros_like(rows)
    return jnp.concatenate([jnp.where(low, rows, zero), jnp.where(low, zero, rows)], 0)


def join_heads(stacked):
    n = stacked.shape[0] // 2
    low = iota((n, LANES), 1) < HALF
    return jnp.where(low, stacked[:n], stacked[n:])


def put_stats(stats, pair, peak, total):
    n = stats.shape[0]
    lane = iota(stats.shape, 1)
    for side in range(2):
        head = 2 * pair + side
        stats = jnp.where(lane == head, peak[side * n:(side + 1) * n], stats)
        stats = jnp.where(lane == STAT + head, total[side * n:(side + 1) * n], stats)
    return stats


def call(body, outs, in_specs, flops, nbytes, grant, scratch=(), space=pltpu.VMEM):
    return pl.pallas_call(
        body,
        scratch_shapes=scratch,
        compiler_params=pltpu.CompilerParams(vmem_limit_bytes=grant << 20),
        out_shape=outs,
        in_specs=in_specs,
        out_specs=[pl.BlockSpec(memory_space=space)] * len(outs),
        cost_estimate=pl.CostEstimate(flops=flops, bytes_accessed=nbytes, transcendentals=0),
    )


def head_row(off_ref, level, shape, per_lane):
    lane = iota(shape, 1)
    lane = lane if per_lane else lane // HALF
    off = jnp.zeros(shape, jnp.int32)
    for head in range(HEADS):
        off = jnp.where(lane == head, off_ref[level, head], off)
    return off


def select_kernel(
    off_hbm, q_hbm, k_hbm, v_hbm, q_ref, k_ref, v_ref, q1_ref, q2_ref, kv1_ref, early_ref, f3_ref, f4_ref, offs_ref, off_ref, pick_ref, sems
):
    pairs = ((off_hbm, off_ref), (q_hbm, q_ref), (k_hbm, k_ref), (v_hbm, v_ref))
    copies = [pltpu.make_async_copy(src, dst, sems.at[n]) for n, (src, dst) in enumerate(pairs)]
    for copy in copies:
        copy.start()
    row = iota((SEL, LANES), 0)
    tok = iota((SEL, LANES), 1)
    base = jnp.where(row < 64, row * 4, jnp.where(row < 80, (row - 64) * 16, (row - 80) * 64))
    base = jnp.where(row < 84, base, jnp.where(row < 85, 0, -4096))
    early_ref[16:24, WIDTH:2 * WIDTH] = jnp.zeros((8, WIDTH), BF16)
    copies[0].wait()
    for head in range(HEADS):
        off = jnp.where(
            row < 64,
            off_ref[1, head],
            jnp.where(row < 80, off_ref[2, head], jnp.where(row < 84, off_ref[3, head], off_ref[4, head])),
        )
        place = base + off
        pick = jnp.concatenate([jnp.where(tok == place, 1.0, 0.0), jnp.where(tok + LANES == place, 1.0, 0.0)], 1)
        pick_ref[SEL * head:SEL * head + SEL, :] = pick.astype(BF16)
    offs_ref[...] = jnp.zeros((8, WIDTH + LANES), jnp.int32)
    for level in range(1, 5):
        offs_ref[level:level + 1, 0:WIDTH] = head_row(off_ref, level, (1, WIDTH), False)
        offs_ref[level:level + 1, WIDTH:WIDTH + LANES] = head_row(off_ref, level, (1, LANES), True)
    for copy in copies[1:]:
        copy.wait()
    for pair in range(PAIRS):
        pick = pick_ref[2 * SEL * pair:2 * SEL * pair + 2 * SEL, :]
        at = lanes_of(pair)
        after = slice(WIDTH + pair * LANES, WIDTH + (pair + 1) * LANES)
        rows = join_heads(dot_nn(pick, q_ref[:, at]) * SCALE).astype(BF16)
        q1_ref[:, at] = rows[0:64]
        q2_ref[:, at] = rows[64:80]
        early_ref[16:24, at] = rows[80:88]
        for ref, here in ((k_ref, at), (v_ref, after)):
            rows = join_heads(dot_nn(pick, ref[:, at])).astype(BF16)
            kv1_ref[:, here] = rows[0:64]
            early_ref[0:16, here] = rows[64:80]
            f3_ref[:, here] = rows[80:84]
            f4_ref[:, here] = rows[84:85]


def local_kernel(q_ref, k_ref, v_ref, acc_ref):
    half = TOK // 2
    for part in range(2):
        keys = (part + 1) * half
        here = slice(part * half, keys)
        query = iota((2 * half, keys), 0) % half + part * half
        allowed = iota((2 * half, keys), 1) <= query
        stats = jnp.zeros((half, LANES), F32)
        for pair in range(PAIRS):
            at = lanes_of(pair)
            queries = split_heads(q_ref[here, at] * jnp.asarray(SCALE, BF16))
            scores = jnp.where(allowed, dot_nt(queries, k_ref[0:keys, at]), NEG)
            peak = jnp.max(scores, axis=1, keepdims=True)
            weights = jnp.exp(scores - peak)
            total = jnp.sum(weights, axis=1, keepdims=True)
            acc_ref[here, at] = join_heads(dot_nn(weights.astype(BF16), v_ref[0:keys, at]))
            stats = put_stats(stats, pair, peak, total)
        acc_ref[here, WIDTH:WIDTH + LANES] = stats


def far_kernel(qa_ref, qb_ref, kf_ref, out_ref):
    me = lax.axis_index("ctx").astype(jnp.int32)

    def device_of(block):
        return me ^ ((block & 1) * 2) ^ (((block >> 1) & 1) * 6) ^ (block >> 2)

    col = iota((1, 128), 1) & 63
    asker = device_of(col >> 3)
    q_row = col & 7
    row = iota((64, 1), 0)
    k_row = row & 7
    owner = (me - (me & 56)) + (row >> 3) * 8
    far_owner = owner ^ ((k_row & 1) * 192) ^ (((k_row >> 1) & 1) * 64)
    third = (owner & 63) * 4 + k_row <= jnp.where(q_row < 4, (asker & 63) * 4 + q_row, -1)
    fourth = far_owner <= jnp.where(q_row == 4, asker, -1)
    allowed = jnp.where(k_row < 4, third.astype(jnp.int32), fourth.astype(jnp.int32)) > 0
    stat_row = iota((32, 64), 0)
    stats = jnp.zeros((32, 64), F32)
    scores = []
    for pair in range(PAIRS):
        at = lanes_of(pair)
        queries = split_heads(jnp.concatenate([qa_ref[:, at], qb_ref[:, at]], 0))
        scores.append(dot_nt(kf_ref[:, at], queries))
    scores = [jnp.where(allowed, score, NEG) for score in scores]
    peaks = [jnp.max(score, axis=0, keepdims=True) for score in scores]
    weights = [jnp.where(allowed, jnp.exp(score - peak), 0.0) for score, peak in zip(scores, peaks)]
    accs = []
    for pair in range(PAIRS):
        vat = slice(WIDTH + pair * LANES, WIDTH + (pair + 1) * LANES)
        accs.append(
            lax.dot_general(
                weights[pair].astype(BF16), kf_ref[:, vat], (((0,), (0,)), ((), ())), preferred_element_type=F32
            )
        )
    totals = [jnp.sum(weight, axis=0, keepdims=True) for weight in weights]
    for pair in range(PAIRS):
        for side in range(2):
            here = slice(64 * side, 64 * side + 64)
            stats = jnp.where(stat_row == 2 * pair + side, peaks[pair][:, here], stats)
            stats = jnp.where(stat_row == STAT + 2 * pair + side, totals[pair][:, here], stats)
    accs = [join_heads(acc).astype(BF16) for acc in accs]
    high = stats.astype(BF16).astype(F32)
    mid = (stats - high).astype(BF16).astype(F32)
    low = stats - high - mid
    stats = jnp.concatenate([high, mid, low, jnp.zeros((32, 64), F32)], 0).T.astype(BF16)
    for number in range(8):
        to = device_of(number) & 7
        here = slice(number * 8, number * 8 + 8)
        for pair in range(PAIRS):
            out_ref[to, :, lanes_of(pair)] = accs[pair][here]
        out_ref[to, :, WIDTH:WIDTH + LANES] = stats[here]


def gathered(q_ref, parts, rows, allowed, together):
    stats = jnp.zeros((rows, LANES), F32)
    accs = []
    for first in range(0, PAIRS, together):
        pairs = range(first, first + together)
        scores = []
        for pair in pairs:
            queries = split_heads(q_ref[:, lanes_of(pair)])
            scores.append(jnp.concatenate([dot_nt(queries, ref[:, lanes_of(pair)]) for ref in parts], 1))
        scores = [jnp.where(allowed, score, NEG) for score in scores]
        peaks = [jnp.max(score, axis=1, keepdims=True) for score in scores]
        weights = [jnp.exp(score - peak) for score, peak in zip(scores, peaks)]
        totals = [jnp.sum(weight, axis=1, keepdims=True) for weight in weights]
        for pair, weight in zip(pairs, weights):
            vat = slice(WIDTH + pair * LANES, WIDTH + (pair + 1) * LANES)
            weight = weight.astype(BF16)
            acc = dot_nn(weight[:, 0:128], parts[0][:, vat]) + dot_nn(weight[:, 128:256], parts[1][:, vat])
            accs.append(join_heads(acc))
        for pair, peak, total in zip(pairs, peaks, totals):
            stats = put_stats(stats, pair, peak, total)
    return accs, stats


def absorb(offs_ref, level, accs, stats, acc_ref, out_ref):
    group = 4**level
    rows = TOK // group
    lane = iota((TOK, LANES), 1)
    tok = iota((TOK, LANES), 0)
    expand = jnp.where((iota((TOK, rows), 0) >> (2 * level)) == iota((TOK, rows), 1), 1.0, 0.0)
    spread = jnp.dot(expand, stats, precision=lax.Precision.HIGHEST, preferred_element_type=F32)
    kept = ((tok & (group - 1)) == offs_ref[level:level + 1, WIDTH:WIDTH + LANES]) & (lane < HEADS)
    stat = acc_ref[:, WIDTH:WIDTH + LANES]
    peak0 = jnp.where(lane < HEADS, stat, 0.0)
    peak1 = jnp.where(kept, spread, NEG)
    best = jnp.maximum(peak0, peak1)
    share0 = jnp.where(lane < HEADS, jnp.exp(peak0 - best), 0.0)
    share1 = jnp.exp(peak1 - best)
    total = share0 * pltpu.roll(stat, LANES - STAT, 1) + share1 * pltpu.roll(spread, LANES - STAT, 1)
    out_ref[:, WIDTH:WIDTH + LANES] = jnp.where(
        lane < HEADS, best, pltpu.roll(jnp.where(lane < HEADS, total, 0.0), STAT, 1)
    )
    row_share = lax.dot_general(
        expand, share1, (((0,), (0,)), ((), ())), precision=lax.Precision.HIGHEST, preferred_element_type=F32
    )
    scale0 = over_lanes(share0)
    scale1 = over_lanes(row_share)
    twice = jnp.concatenate([expand.astype(BF16)] * 2, 1)
    for pair in range(PAIRS):
        at = lanes_of(pair)
        high, low = split2(accs[pair] * scale1[:, at])
        added = dot_nn(twice, jnp.concatenate([high, low], 0))
        off = offs_ref[level:level + 1, at]
        added = jnp.where((iota((TOK, LANES), 0) & (group - 1)) == off, added, 0.0)
        out_ref[:, at] = scale0[:, at] * acc_ref[:, at] + added


def first_kernel(offs_ref, q1_ref, a_ref, b_ref, acc_ref, out_ref):
    me = lax.axis_index("ctx").astype(jnp.int32)
    col = iota((1, TOK), 1)
    device = me ^ (((col >> 6) & 1) * 2) ^ (col >> 7)
    k_pos = (device & 3) * 64 + (col & 63)
    q_pos = (me & 3) * 64 + (iota((128, 1), 0) & 63)
    accs, stats = gathered(q1_ref, (a_ref, b_ref), 64, k_pos <= q_pos, 2)
    absorb(offs_ref, 1, accs, stats, acc_ref, out_ref)


def second_kernel(q2_ref, a_ref, b_ref, out_ref):
    me = lax.axis_index("ctx").astype(jnp.int32)
    col = iota((1, TOK), 1)
    block = (col >> 4) & 3
    device = me ^ ((block & 1) * 2) ^ ((block >> 1) * 6) ^ (((col >> 6) & 1) * 8) ^ (col >> 7)
    k_pos = (device & 15) * 16 + (col & 15)
    q_pos = (me & 15) * 16 + (iota((32, 1), 0) & 15)
    accs, stats = gathered(q2_ref, (a_ref, b_ref), 16, k_pos <= q_pos, 6)
    for pair in range(PAIRS):
        out_ref[:, lanes_of(pair)] = accs[pair]
    out_ref[:, WIDTH:WIDTH + LANES] = stats


def split2(value):
    high = value.astype(BF16)
    return high, (value - high.astype(F32)).astype(BF16)


def over_lanes(coeff):
    high, low = split2(coeff)
    lane = iota((2 * LANES, WIDTH), 1) // HALF
    spread = jnp.where((iota((2 * LANES, WIDTH), 0) & (LANES - 1)) == lane, 1.0, 0.0).astype(BF16)
    return dot_nn(jnp.concatenate([high, low], 1), spread)


def final_kernel(offs_ref, acc_ref, second_ref, ret_ref, out_hbm, out_ref, sems):
    lane = iota((8, LANES), 1)
    parts = []
    for number in range(8):
        stats = ret_ref[number, :, WIDTH:WIDTH + LANES].astype(F32)
        parts.append(stats + pltpu.roll(stats, 96, 1) + pltpu.roll(stats, 64, 1))
    peaks = [jnp.where(lane < HEADS, part, NEG) for part in parts]
    peak = functools.reduce(jnp.maximum, peaks)
    factors = [jnp.where(lane < HEADS, jnp.exp(part - peak), 0.0) for part in peaks]
    total = sum(factor * pltpu.roll(part, LANES - STAT, 1) for factor, part in zip(factors, parts))
    spread = over_lanes(jnp.concatenate(factors, 0))
    rows = sum(
        spread[8 * number:8 * number + 8] * ret_ref[number, :, 0:WIDTH].astype(F32) for number in range(8)
    )
    second = second_ref[:, WIDTH:WIDTH + LANES]
    rows = jnp.concatenate([second_ref[:, 0:WIDTH], rows], 0)
    peak = jnp.concatenate([second, peak], 0)
    total = jnp.concatenate([pltpu.roll(second, LANES - STAT, 1), total], 0)

    def expanded(value, level):
        first = (0, 16, 20)[level - 2]
        group = 4**level
        pieces = [jnp.broadcast_to(value[first + r:first + r + 1], (group, LANES)) for r in range(TOK // group)]
        return jnp.concatenate(pieces, 0)

    lane = iota((TOK, LANES), 1)
    tok = iota((TOK, LANES), 0)
    stat = acc_ref[:, WIDTH:WIDTH + LANES]
    level_peaks = [jnp.where(lane < HEADS, stat, 0.0)]
    level_totals = [pltpu.roll(stat, LANES - STAT, 1)]
    for level in (2, 3, 4):
        kept = ((tok & (4**level - 1)) == offs_ref[level:level + 1, WIDTH:WIDTH + LANES]) & (lane < HEADS)
        level_peaks.append(jnp.where(kept, expanded(peak, level), NEG))
        level_totals.append(expanded(total, level))
    best = functools.reduce(jnp.maximum, level_peaks)
    shares = [jnp.where(lane < HEADS, jnp.exp(value - best), 0.0) for value in level_peaks]
    denom = sum(share * value for share, value in zip(shares, level_totals))
    inverse = 1.0 / jnp.where(lane < HEADS, denom, 1.0)
    shares = [share * inverse for share in shares]
    row_shares = [jnp.sum(shares[1][16 * r:16 * r + 16], axis=0, keepdims=True) for r in range(16)]
    row_shares += [jnp.sum(shares[2][64 * r:64 * r + 64], axis=0, keepdims=True) for r in range(4)]
    row_shares += [jnp.sum(shares[3], axis=0, keepdims=True), jnp.zeros((3, LANES), F32)]
    rows = rows * over_lanes(jnp.concatenate(row_shares, 0))
    scale = over_lanes(shares[0])
    hits = [
        iota((4**level, WIDTH), 0) == offs_ref[level:level + 1, 0:WIDTH] for level in (2, 3, 4)
    ]
    copies = []
    for r in range(16):
        here = slice(16 * r, 16 * r + 16)
        inner = slice(16 * (r % 4), 16 * (r % 4) + 16)
        merged = scale[here] * acc_ref[here, 0:WIDTH]
        merged = merged + jnp.where(hits[0], rows[r:r + 1], 0.0)
        merged = merged + jnp.where(hits[1][inner], rows[16 + r // 4:17 + r // 4], 0.0)
        merged = merged + jnp.where(hits[2][here], rows[20:21], 0.0)
        out_ref[here, :] = merged.astype(BF16)
        if r % 4 == 3:
            done = slice(64 * (r // 4), 64 * (r // 4) + 64)
            copies.append(pltpu.make_async_copy(out_ref.at[done], out_hbm.at[done], sems.at[r // 4]))
            copies[-1].start()
    for copy in copies:
        copy.wait()


def shaped(rows, width, dtype):
    return jax.ShapeDtypeStruct((rows, width), dtype)


def traded(value, mask, count):
    return lax.ppermute(value, "ctx", [(source, source ^ mask) for source in range(count)])


def grown(value, mask, count):
    other = traded(value, mask, count)
    return jnp.concatenate([value, other], 0)


def program(queries, keys, values, offsets):
    count = lax.axis_size("ctx")
    wide = 2 * WIDTH
    inputs = [pltpu.with_memory_space_constraint(a, pltpu.HBM) for a in (offsets, queries, keys, values)]
    q, k, v, q1, q2, kv1, early, third, fourth, places = call(
        select_kernel,
        [shaped(TOK, WIDTH, BF16)] * 3
        + [shaped(64, WIDTH, BF16), shaped(16, WIDTH, BF16), shaped(64, wide, BF16), shaped(24, wide, BF16),
           shaped(4, wide, BF16), shaped(1, wide, BF16), shaped(8, WIDTH + LANES, jnp.int32)],
        [pl.BlockSpec(memory_space=pltpu.HBM)] * 4, 200_000_000, 2_000_000, 12,
        [pltpu.SMEM((5, HEADS), jnp.int32), pltpu.VMEM((HEADS * SEL, TOK), BF16), pltpu.SemaphoreType.DMA((4,))],
    )(*inputs)
    fourth = grown(fourth, 192, count)
    fourth = grown(fourth, 64, count)
    far = jnp.broadcast_to(jnp.concatenate([third, fourth], 0)[None], (8, 8, wide))
    lines = [[first + step for step in range(0, 64, 8)] for first in range(count) if not first & 56]
    far = lax.all_to_all(far, "ctx", 0, 0, axis_index_groups=lines).reshape(64, wide)
    early = grown(early, 2, count)
    early = grown(early, 6, count).reshape(4, 24, wide)
    asked = early[:, 16:24, 0:WIDTH].reshape(32, WIDTH)
    asked_other = traded(asked, 1, count)
    kv1 = grown(kv1, 2, count)
    kv1_other = traded(kv1, 1, count)
    kv2 = grown(early[:, 0:16].reshape(64, wide), 8, count)
    kv2_other = traded(kv2, 1, count)
    total = shaped(TOK, WIDTH + LANES, F32)
    (acc,) = call(local_kernel, [total], [VMEM] * 3, 1_000_000_000, 3_000_000, 12)(q, k, v)
    (acc,) = call(first_kernel, [total], [VMEM] * 5, 600_000_000, 2_000_000, 16)(
        places, q1, kv1, kv1_other, acc
    )
    (partial,) = call(
        far_kernel, [jax.ShapeDtypeStruct((8, 8, WIDTH + LANES), BF16)], [VMEM] * 3,
        200_000_000, 600_000, 12,
    )(asked, asked_other, far)
    groups = [list(range(first, first + 8)) for first in range(0, count, 8)]
    back = lax.all_to_all(partial, "ctx", 0, 0, axis_index_groups=groups)
    (second,) = call(
        second_kernel, [shaped(16, WIDTH + LANES, F32)], [VMEM] * 3, 100_000_000, 900_000, 12
    )(q2, kv2, kv2_other)
    (merged,) = call(
        final_kernel, [shaped(TOK, WIDTH, BF16)], [VMEM] * 4, 1_000_000_000, 3_000_000, 16,
        [pltpu.VMEM((TOK, WIDTH), BF16), pltpu.SemaphoreType.DMA((4,))], pltpu.HBM,
    )(places, acc, second, back)
    return merged


def solution(mesh):
    in_specs = (P("ctx", None), P("ctx", None), P("ctx", None), P())
    return jax.shard_map(program, mesh=mesh, in_specs=in_specs, out_specs=P("ctx", None), check_vma=False)
```

profile of v0, /device:TPU:1, one launch (start us, length us, event | category | flops | bytes accessed | tf_op | source)
XLA Modules:
  0.0 45.6 jit_solution(16011559004291132125)
XLA Ops:
  0.0 1.9 %shard_map.46 = (bf16[256,768]{1,0:T(8,128)(2,1)S(1)}, bf16[256,768]{1,0:T(8,128)(2,1)S(1)}, bf16[256,768]{1,0:T(8,128)(2,1)S(1)}, bf16[64,768]{1,0:T(8,128)(2,1...) custom-call(s32[5,12]{1,0:T(8,128)} %off_hbm.1, ...), custom_call_target="tpu_custom_call" | custom-call | flops 200000000 | bytes 2000000 | tf_op jit(solution)/shard_map/pallas_call | solution.py:374
  1.9 3.6 %collective-permute-start.7 = (bf16[1,1536]{1,0:T(2,128)(2,1)S(1)}, bf16[1,1536]{1,0:T(2,128)(2,1)S(1)}, u32[]{:S(2)}, u32[]{:S(2)}) collective-permute-start(bf16[1,1536]{1,0:T(2,128)(2,1)S(1)} %get-tuple-element.24), channel_id=1, source_target_pairs={{0,192},{1,193},{2,194},{3,195},{4,196},{5,197},{6,198},{7,199},{8... | collective-permute-start | bytes 9224 | tf_op jit(solution)/shard_map/ppermute | solution.py:362
  5.5 1.2 %collective-permute-start.2 = (bf16[24,1536]{1,0:T(8,128)(2,1)S(1)}, bf16[24,1536]{1,0:T(8,128)(2,1)S(1)}, u32[]{:S(2)}, u32[]{:S(2)}) collective-permute-start(bf16[24,1536]{1,0:T(8,128)(2,1)S(1)} %get-tuple-element.22), channel_id=1, source_target_pairs={{0,2},{1,3},{2,0},{3,1},{4,6},{5,7},{6,4},{7,5},{8,10},{9,11},{10,... | collective-permute-start | bytes 221192 | tf_op jit(solution)/shard_map/ppermute | solution.py:362
  6.8 0.3 collective-permute-start
  7.0 0.0 collective-permute-done.7
  7.1 0.1 collective-permute-start.8
  7.2 1.9 %collective-permute-done.2 = bf16[24,1536]{1,0:T(8,128)(2,1)S(1)} collective-permute-done((bf16[24,1536]{1,0:T(8,128)(2,1)S(1)}, bf16[24,1536]{1,0:T(8,128)(2,1)S(1)}, u32[]{:S(2)}, u32[]{:S(2)}) %collective-permute-start.2) | collective-permute-done | bytes 73760 | tf_op jit(solution)/shard_map/ppermute | solution.py:362
  9.1 2.3 %collective-permute-start.3 = (bf16[48,1536]{1,0:T(8,128)(2,1)S(1)}, bf16[48,1536]{1,0:T(8,128)(2,1)S(1)}, u32[]{:S(2)}, u32[]{:S(2)}) collective-permute-start(bf16[48,1536]{1,0:T(8,128)(2,1)S(1)} %pad_maximum_fusion.2), channel_id=1, source_target_pairs={{0,6},{1,7},{2,4},{3,5},{4,2},{5,3},{6,0},{7,1},{8,14},{9,15},{10,... | collective-permute-start | bytes 442376 | tf_op jit(solution)/shard_map/ppermute | solution.py:362
  11.3 0.0 collective-permute-done.8
  11.4 0.7 %broadcast_in_dim.2 = bf16[8,8,1536]{2,1,0:T(8,128)(2,1)} broadcast(bf16[8,1536]{1,0:T(8,128)(2,1)S(1)} %pad_maximum_fusion.3), dimensions={1,2} | broadcast | bytes 221184 | tf_op jit(solution)/shard_map/broadcast_in_dim | solution.py:384
  12.1 8.2 %all-to-all-start = ((bf16[8,8,1536]{2,1,0:T(8,128)(2,1)}), bf16[8,8,1536]{2,1,0:T(8,128)(2,1)S(1)}, u32[]{:S(2)}, u32[]{:S(2)}) async-start(bf16[8,8,1536]{2,1,0:T(8,128)(2,1)} %broadcast_in_dim.2), calls=%async_computation | async-start | bytes 393216 | tf_op jit(solution)/shard_map/all_to_all | solution.py:386
  20.2 0.0 collective-permute-done.3
  20.3 1.5 %collective-permute-start.4 = (bf16[64,1536]{1,0:T(8,128)(2,1)S(1)}, bf16[64,1536]{1,0:T(8,128)(2,1)S(1)}, u32[]{:S(2)}, u32[]{:S(2)}) collective-permute-start(bf16[64,1536]{1,0:T(8,128)(2,1)S(1)} %bitcast.8), channel_id=1, source_target_pairs={{0,8},{1,9},{2,10},{3,11},{4,12},{5,13},{6,14},{7,15},{8,0},{9,1},... | collective-permute-start | bytes 589832 | tf_op jit(solution)/shard_map/ppermute | solution.py:362
  21.8 0.0 collective-permute-done
  21.9 4.1 %collective-permute-start.1 = (bf16[128,1536]{1,0:T(8,128)(2,1)S(1)}, bf16[128,1536]{1,0:T(8,128)(2,1)S(1)}, u32[]{:S(2)}, u32[]{:S(2)}) collective-permute-start(bf16[128,1536]{1,0:T(8,128)(2,1)S(1)} %constant_dynamic-update-slice_fusion.a_ref), channel_id=1, source_target_pairs={{0,1},{1,0},{2,3},{3,2},{4,5},{5,4},{6,7},{7,6},{8,9},{9,8},{10,11... | collective-permute-start | bytes 1179656 | tf_op jit(solution)/shard_map/ppermute | solution.py:362
  26.0 1.6 %collective-permute-done.4 = bf16[64,1536]{1,0:T(8,128)(2,1)S(1)} collective-permute-done((bf16[64,1536]{1,0:T(8,128)(2,1)S(1)}, bf16[64,1536]{1,0:T(8,128)(2,1)S(1)}, u32[]{:S(2)}, u32[]{:S(2)}) %collective-permute-start.4) | collective-permute-done | bytes 196640 | tf_op jit(solution)/shard_map/ppermute | solution.py:362
  27.6 4.5 %collective-permute-start.5 = (bf16[128,1536]{1,0:T(8,128)(2,1)S(1)}, bf16[128,1536]{1,0:T(8,128)(2,1)S(1)}, u32[]{:S(2)}, u32[]{:S(2)}) collective-permute-start(bf16[128,1536]{1,0:T(8,128)(2,1)S(1)} %pad_maximum_fusion.a_ref), channel_id=1, source_target_pairs={{0,1},{1,0},{2,3},{3,2},{4,5},{5,4},{6,7},{7,6},{8,9},{9,8},{10,11... | collective-permute-start | bytes 1179656 | tf_op jit(solution)/shard_map/ppermute | solution.py:362
  32.1 0.1 collective-permute-start.6
  32.2 1.3 %collective-permute-done.6.qb_ref = bf16[32,768]{1,0:T(8,128)(2,1)S(1)} collective-permute-done((bf16[32,768]{1,0:T(8,128)(2,1)S(1)}, bf16[32,768]{1,0:T(8,128)(2,1)S(1)}, u32[]{:S(2)}, u32[]{:S(2)}) %collective-permute-start.6) | collective-permute-done | bytes 49184 | tf_op jit(solution)/shard_map/ppermute | solution.py:362
  33.5 0.0 all-to-all-done
  33.5 1.8 %shard_map.50 = bf16[8,8,896]{2,1,0:T(8,128)(2,1)} custom-call(bf16[32,768]{1,0:T(8,128)(2,1)S(1)} %slice_bitcast_fusion.qa_ref, bf16[32,768]{1,0:T(8,128)(2,1)S(1)} %collective-permute-done.6.qb_ref, bf16[64,1536]{1,0:T(8,128)(2,1)S(1)} %bitcast.5), custom_call_target="tpu_custom_call" | custom-call | flops 200000000 | bytes 600000 | tf_op jit(solution)/shard_map/pallas_call | solution.py:400
  35.3 3.6 %all-to-all-start.1 = ((bf16[8,8,896]{2,1,0:T(8,128)(2,1)}), bf16[8,8,896]{2,1,0:T(8,128)(2,1)S(1)}, u32[]{:S(2)}, u32[]{:S(2)}) async-start(bf16[8,8,896]{2,1,0:T(8,128)(2,1)} %shard_map.50), calls=%async_computation.1 | async-start | bytes 229376 | tf_op jit(solution)/shard_map/all_to_all | solution.py:405
  39.0 1.4 %shard_map.47.acc_ref = f32[256,896]{1,0:T(8,128)S(1)} custom-call(bf16[256,768]{1,0:T(8,128)(2,1)S(1)} %get-tuple-element.18.q_ref, bf16[256,768]{1,0:T(8,128)(2,1)S(1)} %get-tuple-element.19.k_ref, bf16[256,768]{1,0:T(8,128)(2,1)S(1)} %get-tuple-element.20.v_ref), custom_call_target="tpu_custom_call" | custom-call | flops 1000000000 | bytes 3000000 | tf_op jit(solution)/shard_map/pallas_call | solution.py:396
  40.3 0.0 collective-permute-done.1.b_ref
  40.4 2.0 %shard_map.48.acc_ref = f32[256,896]{1,0:T(8,128)S(1)} custom-call(s32[8,896]{1,0:T(8,128)S(1)} %get-tuple-element.15.offs_ref, bf16[64,768]{1,0:T(8,128)(2,1)S(1)} %get-tuple-element.16.q1_ref, bf16[128,1536]{1,0:T(8,128)(2,1)S(1)} %constant_dynamic-update-slice_fusion.a_ref, bf16[128,1536]{1,0:T(8,128)(2,1)S(1)} %collective-permute-done.1.b_ref, ...), custom_call_target="tpu_custom_call" | custom-call | flops 600000000 | bytes 2000000 | tf_op jit(solution)/shard_map/pallas_call | solution.py:397
  42.4 0.0 collective-permute-done.5.b_ref
  42.4 0.5 %shard_map.49.second_ref = f32[16,896]{1,0:T(8,128)S(1)} custom-call(bf16[16,768]{1,0:T(8,128)(2,1)S(1)} %get-tuple-element.21.q2_ref, bf16[128,1536]{1,0:T(8,128)(2,1)S(1)} %pad_maximum_fusion.a_ref, bf16[128,1536]{1,0:T(8,128)(2,1)S(1)} %collective-permute-done.5.b_ref), custom_call_target="tpu_custom_call" | custom-call | flops 100000000 | bytes 900000 | tf_op jit(solution)/shard_map/pallas_call | solution.py:406
  42.9 1.2 %all-to-all-done.1.ret_ref = bf16[8,8,896]{2,1,0:T(8,128)(2,1)S(1)} async-done(((bf16[8,8,896]{2,1,0:T(8,128)(2,1)}), bf16[8,8,896]{2,1,0:T(8,128)(2,1)S(1)}, u32[]{:S(2)}, u32[]{:S(2)}) %all-to-all-start.1) | async-done | bytes 114720 | tf_op jit(solution)/shard_map/all_to_all | solution.py:405
  44.1 1.5 %shard_map.51 = bf16[256,768]{1,0:T(8,128)(2,1)} custom-call(s32[8,896]{1,0:T(8,128)S(1)} %get-tuple-element.15.offs_ref, f32[256,896]{1,0:T(8,128)S(1)} %shard_map.48.acc_ref, f32[16,896]{1,0:T(8,128)S(1)} %shard_map.49.second_ref, bf16[8,8,896]{2,1,0:T(8,128)(2,1)S(1)} %all-to-all-done.1.ret_ref), custom_call_target="tpu_custom_call" | custom-call | flops 1000000000 | bytes 3000000 | tf_op jit(solution)/shard_map/pallas_call | solution.py:409
  (9 shorter events, 0.2 us)
Async XLA Ops:
  1.9 5.1 %collective-permute-start.7 = (bf16[1,1536]{1,0:T(2,128)(2,1)S(1)}, bf16[1,1536]{1,0:T(2,128)(2,1)S(1)}, u32[]{:S(2)}, u32[]{:S(2)}) collective-permute-start(bf16[1,1536]{1,0:T(2,128)(2,1)S(1)} %get-tuple-element.24), channel_id=1, source_target_pairs={{0,192},{1,193},{2,194},{3,195},{4,196},{5,197},{6,198},{7,199},{8... | collective-permute-start | bytes 9224 | tf_op jit(solution)/shard_map/ppermute | solution.py:362
  5.5 3.5 %collective-permute-start.2 = (bf16[24,1536]{1,0:T(8,128)(2,1)S(1)}, bf16[24,1536]{1,0:T(8,128)(2,1)S(1)}, u32[]{:S(2)}, u32[]{:S(2)}) collective-permute-start(bf16[24,1536]{1,0:T(8,128)(2,1)S(1)} %get-tuple-element.22), channel_id=1, source_target_pairs={{0,2},{1,3},{2,0},{3,1},{4,6},{5,7},{6,4},{7,5},{8,10},{9,11},{10,... | collective-permute-start | bytes 221192 | tf_op jit(solution)/shard_map/ppermute | solution.py:362
  6.8 15.1 %collective-permute-start = (bf16[64,1536]{1,0:T(8,128)(2,1)S(1)}, bf16[64,1536]{1,0:T(8,128)(2,1)S(1)}, u32[]{:S(2)}, u32[]{:S(2)}) collective-permute-start(bf16[64,1536]{1,0:T(8,128)(2,1)S(1)} %get-tuple-element.17), channel_id=1, source_target_pairs={{0,2},{1,3},{2,0},{3,1},{4,6},{5,7},{6,4},{7,5},{8,10},{9,11},{10,... | collective-permute-start | bytes 589832 | tf_op jit(solution)/shard_map/ppermute | solution.py:362
  7.1 4.3 %collective-permute-start.8 = (bf16[2,1536]{1,0:T(2,128)(2,1)S(1)}, bf16[2,1536]{1,0:T(2,128)(2,1)S(1)}, u32[]{:S(2)}, u32[]{:S(2)}) collective-permute-start(bf16[2,1536]{1,0:T(2,128)(2,1)S(1)} %pad_maximum_fusion.4), channel_id=1, source_target_pairs={{0,64},{1,65},{2,66},{3,67},{4,68},{5,69},{6,70},{7,71},{8,72},{9,... | collective-permute-start | bytes 18440 | tf_op jit(solution)/shard_map/ppermute | solution.py:362
  9.1 11.2 %collective-permute-start.3 = (bf16[48,1536]{1,0:T(8,128)(2,1)S(1)}, bf16[48,1536]{1,0:T(8,128)(2,1)S(1)}, u32[]{:S(2)}, u32[]{:S(2)}) collective-permute-start(bf16[48,1536]{1,0:T(8,128)(2,1)S(1)} %pad_maximum_fusion.2), channel_id=1, source_target_pairs={{0,6},{1,7},{2,4},{3,5},{4,2},{5,3},{6,0},{7,1},{8,14},{9,15},{10,... | collective-permute-start | bytes 442376 | tf_op jit(solution)/shard_map/ppermute | solution.py:362
  12.1 21.5 %all-to-all-start = ((bf16[8,8,1536]{2,1,0:T(8,128)(2,1)}), bf16[8,8,1536]{2,1,0:T(8,128)(2,1)S(1)}, u32[]{:S(2)}, u32[]{:S(2)}) async-start(bf16[8,8,1536]{2,1,0:T(8,128)(2,1)} %broadcast_in_dim.2), calls=%async_computation | async-start | bytes 393216 | tf_op jit(solution)/shard_map/all_to_all | solution.py:386
  20.3 7.3 %collective-permute-start.4 = (bf16[64,1536]{1,0:T(8,128)(2,1)S(1)}, bf16[64,1536]{1,0:T(8,128)(2,1)S(1)}, u32[]{:S(2)}, u32[]{:S(2)}) collective-permute-start(bf16[64,1536]{1,0:T(8,128)(2,1)S(1)} %bitcast.8), channel_id=1, source_target_pairs={{0,8},{1,9},{2,10},{3,11},{4,12},{5,13},{6,14},{7,15},{8,0},{9,1},... | collective-permute-start | bytes 589832 | tf_op jit(solution)/shard_map/ppermute | solution.py:362
  21.9 18.5 %collective-permute-start.1 = (bf16[128,1536]{1,0:T(8,128)(2,1)S(1)}, bf16[128,1536]{1,0:T(8,128)(2,1)S(1)}, u32[]{:S(2)}, u32[]{:S(2)}) collective-permute-start(bf16[128,1536]{1,0:T(8,128)(2,1)S(1)} %constant_dynamic-update-slice_fusion.a_ref), channel_id=1, source_target_pairs={{0,1},{1,0},{2,3},{3,2},{4,5},{5,4},{6,7},{7,6},{8,9},{9,8},{10,11... | collective-permute-start | bytes 1179656 | tf_op jit(solution)/shard_map/ppermute | solution.py:362
  27.6 14.8 %collective-permute-start.5 = (bf16[128,1536]{1,0:T(8,128)(2,1)S(1)}, bf16[128,1536]{1,0:T(8,128)(2,1)S(1)}, u32[]{:S(2)}, u32[]{:S(2)}) collective-permute-start(bf16[128,1536]{1,0:T(8,128)(2,1)S(1)} %pad_maximum_fusion.a_ref), channel_id=1, source_target_pairs={{0,1},{1,0},{2,3},{3,2},{4,5},{5,4},{6,7},{7,6},{8,9},{9,8},{10,11... | collective-permute-start | bytes 1179656 | tf_op jit(solution)/shard_map/ppermute | solution.py:362
  32.1 1.4 %collective-permute-start.6 = (bf16[32,768]{1,0:T(8,128)(2,1)S(1)}, bf16[32,768]{1,0:T(8,128)(2,1)S(1)}, u32[]{:S(2)}, u32[]{:S(2)}) collective-permute-start(bf16[32,768]{1,0:T(8,128)(2,1)S(1)} %slice_bitcast_fusion.qa_ref), channel_id=1, source_target_pairs={{0,1},{1,0},{2,3},{3,2},{4,5},{5,4},{6,7},{7,6},{8,9},{9,8},{10,11... | collective-permute-start | bytes 147464 | tf_op jit(solution)/shard_map/ppermute | solution.py:362
  35.3 8.8 %all-to-all-start.1 = ((bf16[8,8,896]{2,1,0:T(8,128)(2,1)}), bf16[8,8,896]{2,1,0:T(8,128)(2,1)S(1)}, u32[]{:S(2)}, u32[]{:S(2)}) async-start(bf16[8,8,896]{2,1,0:T(8,128)(2,1)} %shard_map.50), calls=%async_computation.1 | async-start | bytes 229376 | tf_op jit(solution)/shard_map/all_to_all | solution.py:405
where the time goes:
time: 45.9 us; the launch traced here: 45.6 us
  starting transfers between devices  29.5 us (64%)
  Pallas kernels  9.13 us (20%)
  waiting for transfers between devices  5.98 us (13%)
  local copies, waits for them, and re-layouts  0.74 us (2%)
    ppermute x9, starting transfers between devices, traded(): lax.ppermute(value, 'ctx', [(source, source ^ mask) for source in range(c...  17.7 us
    all_to_all x1, starting transfers between devices, program(): lax.all_to_all(far, 'ctx', 0, 0, axis_index_groups=lines).reshape(64, wide)  8.19 us
    ppermute x9, waiting for transfers between devices, traded(): lax.ppermute(value, 'ctx', [(source, source ^ mask) for source in range(c...  4.82 us
    all_to_all x1, starting transfers between devices, program(): back = lax.all_to_all(partial, 'ctx', 0, 0, axis_index_groups=groups)  3.64 us
    pallas_call x1, Pallas kernels, program(): call(first_kernel, [total], [VMEM] * 5, 600000000, 2000000, 16)  2.04 us
    pallas_call x1, Pallas kernels, program(): call(select_kernel, [shaped(TOK, WIDTH, BF16)] * 3 + [shaped(64, WIDTH, B...  1.9 us
    pallas_call x1, Pallas kernels, program(): call(far_kernel, [jax.ShapeDtypeStruct((8, 8, WIDTH + LANES), BF16)], [VM...  1.82 us
    pallas_call x1, Pallas kernels, program(): call(final_kernel, [shaped(TOK, WIDTH, BF16)], [VMEM] * 4, 1000000000, 30...  1.49 us
  transfers between devices with their start and end apart: 11, of which 4 were waited for; matrix products, arithmetic and copies ran while one was open for 2% of the time, Pallas kernels for 13%

commit v1 on v0

--- a/solution.py
+++ b/solution.py
@@ -82,15 +82,46 @@
     return off
 
 
-def select_kernel(
-    off_hbm, q_hbm, k_hbm, v_hbm, q_ref, k_ref, v_ref, q1_ref, q2_ref, kv1_ref, early_ref, f3_ref, f4_ref, offs_ref, off_ref, pick_ref, sems
-):
-    pairs = ((off_hbm, off_ref), (q_hbm, q_ref), (k_hbm, k_ref), (v_hbm, v_ref))
+def start_copies(pairs, sems):
     copies = [pltpu.make_async_copy(src, dst, sems.at[n]) for n, (src, dst) in enumerate(pairs)]
     for copy in copies:
         copy.start()
+    return copies
+
+
+def one_hot(place):
+    tok = iota(place.shape, 1)
+    pick = jnp.concatenate([jnp.where(tok == place, 1.0, 0.0), jnp.where(tok + LANES == place, 1.0, 0.0)], 1)
+    return pick.astype(BF16)
+
+
+def far_select_kernel(off_hbm, k_hbm, v_hbm, k_ref, v_ref, f3_ref, f4_ref, offs_ref, off_ref, sems):
+    copies = start_copies(((off_hbm, off_ref), (k_hbm, k_ref), (v_hbm, v_ref)), sems)
+    row = iota((16, LANES), 0)
+    copies[0].wait()
+    picks = []
+    for head in range(HEADS):
+        place = jnp.where(row < 4, row * 64 + off_ref[3, head], jnp.where(row < 5, off_ref[4, head], -1))
+        picks.append(one_hot(place))
+    offs_ref[...] = jnp.zeros((8, WIDTH + LANES), jnp.int32)
+    for level in range(1, 5):
+        offs_ref[level:level + 1, 0:WIDTH] = head_row(off_ref, level, (1, WIDTH), False)
+        offs_ref[level:level + 1, WIDTH:WIDTH + LANES] = head_row(off_ref, level, (1, LANES), True)
+    for part, ref in enumerate((k_ref, v_ref)):
+        copies[part + 1].wait()
+        for pair in range(PAIRS):
+            pick = jnp.concatenate(picks[2 * pair:2 * pair + 2], 0)
+            rows = join_heads(dot_nn(pick, ref[:, lanes_of(pair)])).astype(BF16)
+            here = slice(part * WIDTH + pair * LANES, part * WIDTH + (pair + 1) * LANES)
+            f3_ref[:, here] = rows[0:4]
+            f4_ref[:, here] = rows[4:5]
+
+
+def near_select_kernel(
+    off_hbm, q_hbm, k_ref, v_ref, q_ref, q1_ref, q2_ref, kv1_ref, early_ref, off_ref, pick_ref, sems
+):
+    copies = start_copies(((off_hbm, off_ref), (q_hbm, q_ref)), sems)
     row = iota((SEL, LANES), 0)
-    tok = iota((SEL, LANES), 1)
     base = jnp.where(row < 64, row * 4, jnp.where(row < 80, (row - 64) * 16, (row - 80) * 64))
     base = jnp.where(row < 84, base, jnp.where(row < 85, 0, -4096))
     early_ref[16:24, WIDTH:2 * WIDTH] = jnp.zeros((8, WIDTH), BF16)
@@ -101,15 +132,8 @@
             off_ref[1, head],
             jnp.where(row < 80, off_ref[2, head], jnp.where(row < 84, off_ref[3, head], off_ref[4, head])),
         )
-        place = base + off
-        pick = jnp.concatenate([jnp.where(tok == place, 1.0, 0.0), jnp.where(tok + LANES == place, 1.0, 0.0)], 1)
-        pick_ref[SEL * head:SEL * head + SEL, :] = pick.astype(BF16)
-    offs_ref[...] = jnp.zeros((8, WIDTH + LANES), jnp.int32)
-    for level in range(1, 5):
-        offs_ref[level:level + 1, 0:WIDTH] = head_row(off_ref, level, (1, WIDTH), False)
-        offs_ref[level:level + 1, WIDTH:WIDTH + LANES] = head_row(off_ref, level, (1, LANES), True)
-    for copy in copies[1:]:
-        copy.wait()
+        pick_ref[SEL * head:SEL * head + SEL, :] = one_hot(base + off)
+    copies[1].wait()
     for pair in range(PAIRS):
         pick = pick_ref[2 * SEL * pair:2 * SEL * pair + 2 * SEL, :]
         at = lanes_of(pair)
@@ -122,8 +146,6 @@
             rows = join_heads(dot_nn(pick, ref[:, at])).astype(BF16)
             kv1_ref[:, here] = rows[0:64]
             early_ref[0:16, here] = rows[64:80]
-            f3_ref[:, here] = rows[80:84]
-            f4_ref[:, here] = rows[84:85]
 
 
 def local_kernel(q_ref, k_ref, v_ref, acc_ref):
@@ -363,22 +385,30 @@
 
 
 def grown(value, mask, count):
-    other = traded(value, mask, count)
-    return jnp.concatenate([value, other], 0)
+    return jnp.concatenate([value, traded(value, mask, count)], 0)
 
 
 def program(queries, keys, values, offsets):
     count = lax.axis_size("ctx")
     wide = 2 * WIDTH
-    inputs = [pltpu.with_memory_space_constraint(a, pltpu.HBM) for a in (offsets, queries, keys, values)]
-    q, k, v, q1, q2, kv1, early, third, fourth, places = call(
-        select_kernel,
-        [shaped(TOK, WIDTH, BF16)] * 3
-        + [shaped(64, WIDTH, BF16), shaped(16, WIDTH, BF16), shaped(64, wide, BF16), shaped(24, wide, BF16),
-           shaped(4, wide, BF16), shaped(1, wide, BF16), shaped(8, WIDTH + LANES, jnp.int32)],
-        [pl.BlockSpec(memory_space=pltpu.HBM)] * 4, 200_000_000, 2_000_000, 12,
-        [pltpu.SMEM((5, HEADS), jnp.int32), pltpu.VMEM((HEADS * SEL, TOK), BF16), pltpu.SemaphoreType.DMA((4,))],
-    )(*inputs)
+    off, queries, keys, values = [
+        pltpu.with_memory_space_constraint(a, pltpu.HBM) for a in (offsets, queries, keys, values)
+    ]
+    hbm = pl.BlockSpec(memory_space=pltpu.HBM)
+    smem = pltpu.SMEM((5, HEADS), jnp.int32)
+    k, v, third, fourth, places = call(
+        far_select_kernel,
+        [shaped(TOK, WIDTH, BF16)] * 2
+        + [shaped(4, wide, BF16), shaped(1, wide, BF16), shaped(8, WIDTH + LANES, jnp.int32)],
+        [hbm] * 3, 50_000_000, 1_000_000, 12, [smem, pltpu.SemaphoreType.DMA((3,))],
+    )(off, keys, values)
+    q, q1, q2, kv1, early = call(
+        near_select_kernel,
+        [shaped(TOK, WIDTH, BF16), shaped(64, WIDTH, BF16), shaped(16, WIDTH, BF16), shaped(64, wide, BF16),
+         shaped(24, wide, BF16)],
+        [hbm] * 2 + [VMEM] * 2, 150_000_000, 1_000_000, 12,
+        [smem, pltpu.VMEM((HEADS * SEL, TOK), BF16), pltpu.SemaphoreType.DMA((2,))],
+    )(off, queries, k, v)
     fourth = grown(fourth, 192, count)
     fourth = grown(fourth, 64, count)
     far = jnp.broadcast_to(jnp.concatenate([third, fourth], 0)[None], (8, 8, wide))

time: 45.9 us -> 48.5 us (1.057)
  waiting for transfers between devices: 5.98 us -> 8.57 us
  starting transfers between devices: 29.5 us -> 28.4 us
  Pallas kernels: 9.13 us -> 10.2 us
    ppermute x9, waiting for transfers between devices: 4.82 us -> 7.39 us  [traded(): lax.ppermute(value, 'ctx', [(source, source ^ mask) for source in range(c...]
    pallas_call x1 -> x2, Pallas kernels: 1.9 us -> 3.04 us  [the longest x1 1.63 us: program(): call(near_select_kernel, [shaped(TOK, WIDTH, BF16), shaped(64, WIDTH, BF1...]
    ppermute x9, starting transfers between devices: 17.7 us -> 16.6 us  [traded(): lax.ppermute(value, 'ctx', [(source, source ^ mask) for source in range(c...]
  transfers between devices with their start and end apart: 11 -> 11, of which waited for: 4 -> 5; matrix products, arithmetic and copies ran while one was open for 2% -> 2% of each run, Pallas kernels for 13% -> 12%
where the time goes in v1:
time: 48.5 us; the launch traced here: 48.2 us
  starting transfers between devices  28.4 us (59%)
  Pallas kernels  10.2 us (21%)
  waiting for transfers between devices  8.57 us (18%)
  local copies, waits for them, and re-layouts  0.74 us (2%)
    ppermute x9, starting transfers between devices, traded(): lax.ppermute(value, 'ctx', [(source, source ^ mask) for source in range(c...  16.6 us
    all_to_all x1, starting transfers between devices, program(): lax.all_to_all(far, 'ctx', 0, 0, axis_index_groups=lines).reshape(64, wide)  8.2 us
    ppermute x9, waiting for transfers between devices, traded(): lax.ppermute(value, 'ctx', [(source, source ^ mask) for source in range(c...  7.39 us
    all_to_all x1, starting transfers between devices, program(): back = lax.all_to_all(partial, 'ctx', 0, 0, axis_index_groups=groups)  3.64 us
    pallas_call x1, Pallas kernels, program(): call(first_kernel, [total], [VMEM] * 5, 600000000, 2000000, 16)  2.04 us
    pallas_call x1, Pallas kernels, program(): call(far_kernel, [jax.ShapeDtypeStruct((8, 8, WIDTH + LANES), BF16)], [VM...  1.82 us
    pallas_call x1, Pallas kernels, program(): call(near_select_kernel, [shaped(TOK, WIDTH, BF16), shaped(64, WIDTH, BF1...  1.63 us
    pallas_call x1, Pallas kernels, program(): call(final_kernel, [shaped(TOK, WIDTH, BF16)], [VMEM] * 4, 1000000000, 30...  1.49 us
  transfers between devices with their start and end apart: 11, of which 5 were waited for; matrix products, arithmetic and copies ran while one was open for 2% of the time, Pallas kernels for 12%

profile of v1, /device:TPU:1, one launch (start us, length us, event | category | flops | bytes accessed | tf_op | source)
XLA Modules:
  0.0 48.2 jit_solution(10617166968848933463)
XLA Ops:
  0.0 1.4 %shard_map.46 = (bf16[256,768]{1,0:T(8,128)(2,1)S(1)}, bf16[256,768]{1,0:T(8,128)(2,1)S(1)}, bf16[4,1536]{1,0:T(4,128)(2,1)S(1)}, bf16[1,1536]{1,0:T(2,128)(2,1)S(1)}, s32[8,896]{1,0:T(8,128)S(1)}) custom-call(s32[5,12]{1,0:T(8,128)} %off_hbm.3, bf16[256,768]{1,0:T(8,128)(2,1)} %k_hbm.1, bf16[256,768]{1,0:T(8,128)(2,1)} %v_hbm.1), custom_call_target="tpu_custom_call" | custom-call | flops 50000000 | bytes 1000000 | tf_op jit(solution)/shard_map/pallas_call | solution.py:399
  1.4 1.6 %shard_map.47 = (bf16[256,768]{1,0:T(8,128)(2,1)S(1)}, bf16[64,768]{1,0:T(8,128)(2,1)S(1)}, bf16[16,768]{1,0:T(8,128)(2,1)S(1)}, bf16[64,1536]{1,0:T(8,128)(2,1)S(1)}, bf16[24,1536]{1,0:T(8,128)(2,1)S(1)}) custom-call(s32[5,12]{1,0:T(8,128)} %off_hbm.3, bf16[256,768]{1,0:T(8,128)(2,1)} %q_hbm.1, bf16[256,768]{1,0:T(8,128)(2,1)S(1)} %get-tuple-element.16.k_ref, ...), custom_call_target="tpu_custom_call" | custom-call | flops 150000000 | bytes 1000000 | tf_op jit(solution)/shard_map/pallas_call | solution.py:405
  3.1 2.1 %collective-permute-start = (bf16[64,1536]{1,0:T(8,128)(2,1)S(1)}, bf16[64,1536]{1,0:T(8,128)(2,1)S(1)}, u32[]{:S(2)}, u32[]{:S(2)}) collective-permute-start(bf16[64,1536]{1,0:T(8,128)(2,1)S(1)} %get-tuple-element.19), channel_id=1, source_target_pairs={{0,2},{1,3},{2,0},{3,1},{4,6},{5,7},{6,4},{7,5},{8,10},{9,11},{10,... | collective-permute-start | bytes 589832 | tf_op jit(solution)/shard_map/ppermute | solution.py:384
  5.2 0.1 collective-permute-start.2
  5.3 2.9 %collective-permute-start.7 = (bf16[1,1536]{1,0:T(2,128)(2,1)S(1)}, bf16[1,1536]{1,0:T(2,128)(2,1)S(1)}, u32[]{:S(2)}, u32[]{:S(2)}) collective-permute-start(bf16[1,1536]{1,0:T(2,128)(2,1)S(1)} %get-tuple-element.24), channel_id=1, source_target_pairs={{0,192},{1,193},{2,194},{3,195},{4,196},{5,197},{6,198},{7,199},{8... | collective-permute-start | bytes 9224 | tf_op jit(solution)/shard_map/ppermute | solution.py:384
  8.2 1.0 %collective-permute-done.7 = bf16[1,1536]{1,0:T(2,128)(2,1)S(1)} collective-permute-done((bf16[1,1536]{1,0:T(2,128)(2,1)S(1)}, bf16[1,1536]{1,0:T(2,128)(2,1)S(1)}, u32[]{:S(2)}, u32[]{:S(2)}) %collective-permute-start.7) | collective-permute-done | bytes 3104 | tf_op jit(solution)/shard_map/ppermute | solution.py:384
  9.2 0.4 collective-permute-start.8
  9.6 0.5 %collective-permute-done.2 = bf16[24,1536]{1,0:T(8,128)(2,1)S(1)} collective-permute-done((bf16[24,1536]{1,0:T(8,128)(2,1)S(1)}, bf16[24,1536]{1,0:T(8,128)(2,1)S(1)}, u32[]{:S(2)}, u32[]{:S(2)}) %collective-permute-start.2) | collective-permute-done | bytes 73760 | tf_op jit(solution)/shard_map/ppermute | solution.py:384
  10.1 3.8 %collective-permute-start.3 = (bf16[48,1536]{1,0:T(8,128)(2,1)S(1)}, bf16[48,1536]{1,0:T(8,128)(2,1)S(1)}, u32[]{:S(2)}, u32[]{:S(2)}) collective-permute-start(bf16[48,1536]{1,0:T(8,128)(2,1)S(1)} %pad_maximum_fusion.2), channel_id=1, source_target_pairs={{0,6},{1,7},{2,4},{3,5},{4,2},{5,3},{6,0},{7,1},{8,14},{9,15},{10,... | collective-permute-start | bytes 442376 | tf_op jit(solution)/shard_map/ppermute | solution.py:384
  13.9 0.0 collective-permute-done.8
  13.9 0.7 %broadcast_in_dim.2 = bf16[8,8,1536]{2,1,0:T(8,128)(2,1)} broadcast(bf16[8,1536]{1,0:T(8,128)(2,1)S(1)} %pad_maximum_fusion.3), dimensions={1,2} | broadcast | bytes 221184 | tf_op jit(solution)/shard_map/broadcast_in_dim | solution.py:414
  14.6 8.2 %all-to-all-start = ((bf16[8,8,1536]{2,1,0:T(8,128)(2,1)}), bf16[8,8,1536]{2,1,0:T(8,128)(2,1)S(1)}, u32[]{:S(2)}, u32[]{:S(2)}) async-start(bf16[8,8,1536]{2,1,0:T(8,128)(2,1)} %broadcast_in_dim.2), calls=%async_computation | async-start | bytes 393216 | tf_op jit(solution)/shard_map/all_to_all | solution.py:416
  22.8 0.0 collective-permute-done.3
  22.9 1.5 %collective-permute-start.4 = (bf16[64,1536]{1,0:T(8,128)(2,1)S(1)}, bf16[64,1536]{1,0:T(8,128)(2,1)S(1)}, u32[]{:S(2)}, u32[]{:S(2)}) collective-permute-start(bf16[64,1536]{1,0:T(8,128)(2,1)S(1)} %bitcast.8), channel_id=1, source_target_pairs={{0,8},{1,9},{2,10},{3,11},{4,12},{5,13},{6,14},{7,15},{8,0},{9,1},... | collective-permute-start | bytes 589832 | tf_op jit(solution)/shard_map/ppermute | solution.py:384
  24.4 0.0 collective-permute-done
  24.5 2.7 %collective-permute-start.1 = (bf16[128,1536]{1,0:T(8,128)(2,1)S(1)}, bf16[128,1536]{1,0:T(8,128)(2,1)S(1)}, u32[]{:S(2)}, u32[]{:S(2)}) collective-permute-start(bf16[128,1536]{1,0:T(8,128)(2,1)S(1)} %constant_dynamic-update-slice_fusion.a_ref), channel_id=1, source_target_pairs={{0,1},{1,0},{2,3},{3,2},{4,5},{5,4},{6,7},{7,6},{8,9},{9,8},{10,11... | collective-permute-start | bytes 1179656 | tf_op jit(solution)/shard_map/ppermute | solution.py:384
  27.2 4.6 %collective-permute-done.4 = bf16[64,1536]{1,0:T(8,128)(2,1)S(1)} collective-permute-done((bf16[64,1536]{1,0:T(8,128)(2,1)S(1)}, bf16[64,1536]{1,0:T(8,128)(2,1)S(1)}, u32[]{:S(2)}, u32[]{:S(2)}) %collective-permute-start.4) | collective-permute-done | bytes 196640 | tf_op jit(solution)/shard_map/ppermute | solution.py:384
  31.8 2.9 %collective-permute-start.5 = (bf16[128,1536]{1,0:T(8,128)(2,1)S(1)}, bf16[128,1536]{1,0:T(8,128)(2,1)S(1)}, u32[]{:S(2)}, u32[]{:S(2)}) collective-permute-start(bf16[128,1536]{1,0:T(8,128)(2,1)S(1)} %pad_maximum_fusion.a_ref), channel_id=1, source_target_pairs={{0,1},{1,0},{2,3},{3,2},{4,5},{5,4},{6,7},{7,6},{8,9},{9,8},{10,11... | collective-permute-start | bytes 1179656 | tf_op jit(solution)/shard_map/ppermute | solution.py:384
  34.7 0.1 collective-permute-start.6
  34.8 1.3 %collective-permute-done.6.qb_ref = bf16[32,768]{1,0:T(8,128)(2,1)S(1)} collective-permute-done((bf16[32,768]{1,0:T(8,128)(2,1)S(1)}, bf16[32,768]{1,0:T(8,128)(2,1)S(1)}, u32[]{:S(2)}, u32[]{:S(2)}) %collective-permute-start.6) | collective-permute-done | bytes 49184 | tf_op jit(solution)/shard_map/ppermute | solution.py:384
  36.1 0.0 all-to-all-done
  36.1 1.8 %shard_map.51 = bf16[8,8,896]{2,1,0:T(8,128)(2,1)} custom-call(bf16[32,768]{1,0:T(8,128)(2,1)S(1)} %slice_bitcast_fusion.qa_ref, bf16[32,768]{1,0:T(8,128)(2,1)S(1)} %collective-permute-done.6.qb_ref, bf16[64,1536]{1,0:T(8,128)(2,1)S(1)} %bitcast.5), custom_call_target="tpu_custom_call" | custom-call | flops 200000000 | bytes 600000 | tf_op jit(solution)/shard_map/pallas_call | solution.py:430
  37.9 3.6 %all-to-all-start.1 = ((bf16[8,8,896]{2,1,0:T(8,128)(2,1)}), bf16[8,8,896]{2,1,0:T(8,128)(2,1)S(1)}, u32[]{:S(2)}, u32[]{:S(2)}) async-start(bf16[8,8,896]{2,1,0:T(8,128)(2,1)} %shard_map.51), calls=%async_computation.1 | async-start | bytes 229376 | tf_op jit(solution)/shard_map/all_to_all | solution.py:435
  41.6 1.3 %shard_map.48.acc_ref = f32[256,896]{1,0:T(8,128)S(1)} custom-call(bf16[256,768]{1,0:T(8,128)(2,1)S(1)} %get-tuple-element.20.q_ref, bf16[256,768]{1,0:T(8,128)(2,1)S(1)} %get-tuple-element.16.k_ref, bf16[256,768]{1,0:T(8,128)(2,1)S(1)} %get-tuple-element.17.v_ref), custom_call_target="tpu_custom_call" | custom-call | flops 1000000000 | bytes 3000000 | tf_op jit(solution)/shard_map/pallas_call | solution.py:426
  42.9 0.0 collective-permute-done.1.b_ref
  42.9 2.0 %shard_map.49.acc_ref = f32[256,896]{1,0:T(8,128)S(1)} custom-call(s32[8,896]{1,0:T(8,128)S(1)} %get-tuple-element.15.offs_ref, bf16[64,768]{1,0:T(8,128)(2,1)S(1)} %get-tuple-element.18.q1_ref, bf16[128,1536]{1,0:T(8,128)(2,1)S(1)} %constant_dynamic-update-slice_fusion.a_ref, bf16[128,1536]{1,0:T(8,128)(2,1)S(1)} %collective-permute-done.1.b_ref, ...), custom_call_target="tpu_custom_call" | custom-call | flops 600000000 | bytes 2000000 | tf_op jit(solution)/shard_map/pallas_call | solution.py:427
  45.0 0.0 collective-permute-done.5.b_ref
  45.0 0.5 %shard_map.50.second_ref = f32[16,896]{1,0:T(8,128)S(1)} custom-call(bf16[16,768]{1,0:T(8,128)(2,1)S(1)} %get-tuple-element.21.q2_ref, bf16[128,1536]{1,0:T(8,128)(2,1)S(1)} %pad_maximum_fusion.a_ref, bf16[128,1536]{1,0:T(8,128)(2,1)S(1)} %collective-permute-done.5.b_ref), custom_call_target="tpu_custom_call" | custom-call | flops 100000000 | bytes 900000 | tf_op jit(solution)/shard_map/pallas_call | solution.py:436
  45.5 1.2 %all-to-all-done.1.ret_ref = bf16[8,8,896]{2,1,0:T(8,128)(2,1)S(1)} async-done(((bf16[8,8,896]{2,1,0:T(8,128)(2,1)}), bf16[8,8,896]{2,1,0:T(8,128)(2,1)S(1)}, u32[]{:S(2)}, u32[]{:S(2)}) %all-to-all-start.1) | async-done | bytes 114720 | tf_op jit(solution)/shard_map/all_to_all | solution.py:435
  46.7 1.5 %shard_map.52 = bf16[256,768]{1,0:T(8,128)(2,1)} custom-call(s32[8,896]{1,0:T(8,128)S(1)} %get-tuple-element.15.offs_ref, f32[256,896]{1,0:T(8,128)S(1)} %shard_map.49.acc_ref, f32[16,896]{1,0:T(8,128)S(1)} %shard_map.50.second_ref, bf16[8,8,896]{2,1,0:T(8,128)(2,1)S(1)} %all-to-all-done.1.ret_ref), custom_call_target="tpu_custom_call" | custom-call | flops 1000000000 | bytes 3000000 | tf_op jit(solution)/shard_map/pallas_call | solution.py:439
  (9 shorter events, 0.2 us)
Async XLA Ops:
  3.1 21.4 %collective-permute-start = (bf16[64,1536]{1,0:T(8,128)(2,1)S(1)}, bf16[64,1536]{1,0:T(8,128)(2,1)S(1)}, u32[]{:S(2)}, u32[]{:S(2)}) collective-permute-start(bf16[64,1536]{1,0:T(8,128)(2,1)S(1)} %get-tuple-element.19), channel_id=1, source_target_pairs={{0,2},{1,3},{2,0},{3,1},{4,6},{5,7},{6,4},{7,5},{8,10},{9,11},{10,... | collective-permute-start | bytes 589832 | tf_op jit(solution)/shard_map/ppermute | solution.py:384
  5.2 4.9 %collective-permute-start.2 = (bf16[24,1536]{1,0:T(8,128)(2,1)S(1)}, bf16[24,1536]{1,0:T(8,128)(2,1)S(1)}, u32[]{:S(2)}, u32[]{:S(2)}) collective-permute-start(bf16[24,1536]{1,0:T(8,128)(2,1)S(1)} %get-tuple-element.22), channel_id=1, source_target_pairs={{0,2},{1,3},{2,0},{3,1},{4,6},{5,7},{6,4},{7,5},{8,10},{9,11},{10,... | collective-permute-start | bytes 221192 | tf_op jit(solution)/shard_map/ppermute | solution.py:384
  5.3 3.9 %collective-permute-start.7 = (bf16[1,1536]{1,0:T(2,128)(2,1)S(1)}, bf16[1,1536]{1,0:T(2,128)(2,1)S(1)}, u32[]{:S(2)}, u32[]{:S(2)}) collective-permute-start(bf16[1,1536]{1,0:T(2,128)(2,1)S(1)} %get-tuple-element.24), channel_id=1, source_target_pairs={{0,192},{1,193},{2,194},{3,195},{4,196},{5,197},{6,198},{7,199},{8... | collective-permute-start | bytes 9224 | tf_op jit(solution)/shard_map/ppermute | solution.py:384
  9.2 4.7 %collective-permute-start.8 = (bf16[2,1536]{1,0:T(2,128)(2,1)S(1)}, bf16[2,1536]{1,0:T(2,128)(2,1)S(1)}, u32[]{:S(2)}, u32[]{:S(2)}) collective-permute-start(bf16[2,1536]{1,0:T(2,128)(2,1)S(1)} %pad_maximum_fusion.4), channel_id=1, source_target_pairs={{0,64},{1,65},{2,66},{3,67},{4,68},{5,69},{6,70},{7,71},{8,72},{9,... | collective-permute-start | bytes 18440 | tf_op jit(solution)/shard_map/ppermute | solution.py:384
  10.1 12.7 %collective-permute-start.3 = (bf16[48,1536]{1,0:T(8,128)(2,1)S(1)}, bf16[48,1536]{1,0:T(8,128)(2,1)S(1)}, u32[]{:S(2)}, u32[]{:S(2)}) collective-permute-start(bf16[48,1536]{1,0:T(8,128)(2,1)S(1)} %pad_maximum_fusion.2), channel_id=1, source_target_pairs={{0,6},{1,7},{2,4},{3,5},{4,2},{5,3},{6,0},{7,1},{8,14},{9,15},{10,... | collective-permute-start | bytes 442376 | tf_op jit(solution)/shard_map/ppermute | solution.py:384
  14.6 21.5 %all-to-all-start = ((bf16[8,8,1536]{2,1,0:T(8,128)(2,1)}), bf16[8,8,1536]{2,1,0:T(8,128)(2,1)S(1)}, u32[]{:S(2)}, u32[]{:S(2)}) async-start(bf16[8,8,1536]{2,1,0:T(8,128)(2,1)} %broadcast_in_dim.2), calls=%async_computation | async-start | bytes 393216 | tf_op jit(solution)/shard_map/all_to_all | solution.py:416
  22.9 8.9 %collective-permute-start.4 = (bf16[64,1536]{1,0:T(8,128)(2,1)S(1)}, bf16[64,1536]{1,0:T(8,128)(2,1)S(1)}, u32[]{:S(2)}, u32[]{:S(2)}) collective-permute-start(bf16[64,1536]{1,0:T(8,128)(2,1)S(1)} %bitcast.8), channel_id=1, source_target_pairs={{0,8},{1,9},{2,10},{3,11},{4,12},{5,13},{6,14},{7,15},{8,0},{9,1},... | collective-permute-start | bytes 589832 | tf_op jit(solution)/shard_map/ppermute | solution.py:384
  24.5 18.5 %collective-permute-start.1 = (bf16[128,1536]{1,0:T(8,128)(2,1)S(1)}, bf16[128,1536]{1,0:T(8,128)(2,1)S(1)}, u32[]{:S(2)}, u32[]{:S(2)}) collective-permute-start(bf16[128,1536]{1,0:T(8,128)(2,1)S(1)} %constant_dynamic-update-slice_fusion.a_ref), channel_id=1, source_target_pairs={{0,1},{1,0},{2,3},{3,2},{4,5},{5,4},{6,7},{7,6},{8,9},{9,8},{10,11... | collective-permute-start | bytes 1179656 | tf_op jit(solution)/shard_map/ppermute | solution.py:384
  31.8 13.2 %collective-permute-start.5 = (bf16[128,1536]{1,0:T(8,128)(2,1)S(1)}, bf16[128,1536]{1,0:T(8,128)(2,1)S(1)}, u32[]{:S(2)}, u32[]{:S(2)}) collective-permute-start(bf16[128,1536]{1,0:T(8,128)(2,1)S(1)} %pad_maximum_fusion.a_ref), channel_id=1, source_target_pairs={{0,1},{1,0},{2,3},{3,2},{4,5},{5,4},{6,7},{7,6},{8,9},{9,8},{10,11... | collective-permute-start | bytes 1179656 | tf_op jit(solution)/shard_map/ppermute | solution.py:384
  34.7 1.4 %collective-permute-start.6 = (bf16[32,768]{1,0:T(8,128)(2,1)S(1)}, bf16[32,768]{1,0:T(8,128)(2,1)S(1)}, u32[]{:S(2)}, u32[]{:S(2)}) collective-permute-start(bf16[32,768]{1,0:T(8,128)(2,1)S(1)} %slice_bitcast_fusion.qa_ref), channel_id=1, source_target_pairs={{0,1},{1,0},{2,3},{3,2},{4,5},{5,4},{6,7},{7,6},{8,9},{9,8},{10,11... | collective-permute-start | bytes 147464 | tf_op jit(solution)/shard_map/ppermute | solution.py:384
  37.9 8.8 %all-to-all-start.1 = ((bf16[8,8,896]{2,1,0:T(8,128)(2,1)}), bf16[8,8,896]{2,1,0:T(8,128)(2,1)S(1)}, u32[]{:S(2)}, u32[]{:S(2)}) async-start(bf16[8,8,896]{2,1,0:T(8,128)(2,1)} %shard_map.51), calls=%async_computation.1 | async-start | bytes 229376 | tf_op jit(solution)/shard_map/all_to_all | solution.py:435
